TPU v7x, 256 devices: a whole 4x4x8 slice. The times are simulated.
256 devices in a mesh: section: 8 (over z), dp: 32 (over y, x, core).
Axes of the slice: x: 4, y: 4, z: 8, core: 2. Of those that a mesh axis runs over, the one named last changes fastest.
Arguments:
- section_inputs: bfloat16 [8, 8192, 896], P('section', 'dp'), may hold values from -44 to 44
- cotangent: bfloat16 [8192, 896], P('dp'), may hold values from -6 to 6
- norm_gain: float32 [8, 896], P('section'), may hold values from 0.25 to 1.75
- quant_gate: bfloat16 [8, 896, 2432], P('section', 'dp'), may hold values from -1 to 1
- quant_up: bfloat16 [8, 896, 2432], P('section', 'dp'), may hold values from -1 to 1
- scales: float32 [8, 2], P('section'), may hold values from 0.04 to 0.08
- down_proj: bfloat16 [8, 2432, 896], P('section'), may hold values from -0.125 to 0.125
- master_gate: float32 [8, 896, 2432], P('section', 'dp'), may hold values from -0.3 to 0.3
- master_up: float32 [8, 896, 2432], P('section', 'dp'), may hold values from -0.3 to 0.3
- moment_gate: float32 [8, 896, 2432], P('section', 'dp'), may hold values from -3 to 3
- moment_up: float32 [8, 896, 2432], P('section', 'dp'), may hold values from -3 to 3
- second_gate: float32 [8, 896, 2432], P('section', 'dp'), may hold values from 0.05 to 1
- second_up: float32 [8, 896, 2432], P('section', 'dp'), may hold values from 0.05 to 1
- next_inputs: bfloat16 [8, 8192, 896], P('section', 'dp'), may hold values from -44 to 44
Outputs:
- input_grads: bfloat16 [8, 8192, 896], P('section', 'dp')
- master_gate_new: float32 [8, 896, 2432], P('section', 'dp')
- master_up_new: float32 [8, 896, 2432], P('section', 'dp')
- moment_gate_new: float32 [8, 896, 2432], P('section', 'dp')
- moment_up_new: float32 [8, 896, 2432], P('section', 'dp')
- second_gate_new: float32 [8, 896, 2432], P('section', 'dp')
- second_up_new: float32 [8, 896, 2432], P('section', 'dp')
- new_scales: float32 [8, 2], P('section')
- next_hidden: bfloat16 [8, 8192, 2432], P('section', 'dp')
All inputs are finite; a program needn't handle non-finite values. Where the computation divides by a largest or mean magnitude, that divisor is 1e-20 or more.
Results may differ from a plain program's by a relative error of at most 0.034.
Values may be sent and summed in bfloat16 or wider, within the bound.
A program may use at most 128 MiB of HBM per device.

v0:
```python
import functools
import jax
import jax.numpy as jnp
from jax import lax
from jax.experimental import pallas as pl
from jax.experimental.pallas import tpu as pltpu
from jax.sharding import PartitionSpec as P

beta_one = 0.9
beta_two = 0.95
learn_rate = 0.002
decay_rate = 0.1
adam_steps = 100.0
norm_eps = 1e-06
adam_eps = 1e-08
scale_eps = 1e-06

RING = 4
CORES = 2
ROWS = 28
PAD = 32
PARTS = (64, 64, 64, 64)
F32 = jnp.float32
BF16 = jnp.bfloat16
NT = (((1,), (1,)), ((), ()))
NN = (((1,), (0,)), ((), ()))


def mm(a, b, dims=NN):
    return lax.dot_general(a, b, dims, preferred_element_type=F32)


def tiles(count, step=512):
    return [(i, min(step, count - i)) for i in range(0, count, step)]


def coords():
    dp = lax.axis_index("dp")
    chip = dp // CORES
    return chip // RING, chip % RING, dp % CORES


def dp_index(y, x, core):
    return (y * RING + x) * CORES + core


class Copies:
    def __init__(self, send_sem, recv_sem):
        self.send_sem, self.recv_sem = send_sem, recv_sem
        self.sent = []
        self.slots = {}

    def slot(self, key):
        return self.slots.setdefault(key, len(self.slots))

    def start(self, src, dst, key, device):
        copy = pltpu.make_async_remote_copy(
            src_ref=src,
            dst_ref=dst,
            send_sem=self.send_sem.at[len(self.sent)],
            recv_sem=self.recv_sem.at[self.slot(key)],
            device_id={"dp": device},
            device_id_type=pl.DeviceIdType.MESH,
        )
        copy.start()
        self.sent.append(copy)

    def wait_recv(self, dst, key):
        pltpu.make_async_remote_copy(
            src_ref=dst,
            dst_ref=dst,
            send_sem=self.send_sem.at[0],
            recv_sem=self.recv_sem.at[self.slot(key)],
            device_id={"dp": lax.axis_index("dp")},
            device_id_type=pl.DeviceIdType.MESH,
        ).wait_recv()

    def wait_sends(self):
        for copy in self.sent:
            copy.wait_send()


def plane_barrier(extra=()):
    y, x, core = coords()
    sem = pltpu.get_barrier_semaphore()
    for device in (
        dp_index((y + 1) % RING, x, core),
        dp_index((y + RING - 1) % RING, x, core),
        dp_index(y, (x + 1) % RING, core),
        dp_index(y, (x + RING - 1) % RING, core),
        dp_index(y, x, 1 - core),
    ):
        pl.semaphore_signal(sem, inc=1, device_id={"dp": device}, device_id_type=pl.DeviceIdType.MESH)
    for section in extra:
        pl.semaphore_signal(sem, inc=1, device_id={"section": section}, device_id_type=pl.DeviceIdType.MESH)
    pl.semaphore_wait(sem, 5 + len(extra))


def gather_steps(buf, copies, hidden):
    y, x, core = coords()

    def place(half, first, second):
        if half == 0:
            return (y + second) % RING, (x + first) % RING
        return (y + first) % RING, (x + second) % RING

    def piece(half, first, second, which, owner_core=None):
        py, px = place(half, first, second)
        base = dp_index(py, px, core if owner_core is None else owner_core) * PAD
        start, size = {None: (0, PAD), 0: (0, PAD // 2), 1: (PAD // 2, PAD // 2)}[which]
        start = pl.multiple_of(base + start, PAD // 2)
        return buf.at[pl.ds(start, size), pl.ds(half * hidden, hidden)]

    def send(half, first, second, which, axis, step):
        if axis == 0:
            py, px = place(half, step, 0)
            key = ("ag", half, (first - step) % RING, second, which)
        else:
            py, px = place(half, 0, step)
            key = ("ag", half, first, (second - step) % RING, which)
        ref = piece(half, first, second, which)
        copies.start(ref, ref, key, dp_index(py, px, core))

    def sibling(half, first, second):
        ref = piece(half, first, second, None)
        copies.start(ref, ref, ("sib", half, first, second), dp_index(y, x, 1 - core))

    def arrive(half, first, second):
        for which in (0, 1) if 2 in (first if second == 0 else second,) else (None,):
            copies.wait_recv(piece(half, first, second, which), ("ag", half, first, second, which))

    def spread(half, first):
        send(half, first, 0, None, 1, 1)
        send(half, first, 0, None, 1, -1)

    def on_first(half, first):
        arrive(half, first, 0)
        if first == 3:
            send(half, first, 0, 0, 0, 1)
        if first == 1:
            send(half, first, 0, 1, 0, -1)
        spread(half, first)
        sibling(half, first, 0)

    def on_second(half, first, second):
        arrive(half, first, second)
        if second == 3:
            send(half, first, second, 0, 1, 1)
        if second == 1:
            send(half, first, second, 1, 1, -1)
        sibling(half, first, second)

    def begin(half):
        send(half, 0, 0, None, 0, 1)
        send(half, 0, 0, None, 0, -1)
        spread(half, 0)
        sibling(half, 0, 0)

    def both(step, *key):
        return [functools.partial(step, half, *key) for half in (0, 1)]

    rounds = (
        both(on_first, 3) + both(on_first, 1),
        both(on_second, 0, 3) + both(on_second, 0, 1) + both(on_first, 2),
        both(on_second, 0, 2),
        both(on_second, 3, 3) + both(on_second, 3, 1) + both(on_second, 1, 3) + both(on_second, 1, 1),
        both(on_second, 3, 2) + both(on_second, 1, 2),
        both(on_second, 2, 3) + both(on_second, 2, 1),
        both(on_second, 2, 2),
    )

    def from_sibling(half, first, second):
        copies.wait_recv(piece(half, first, second, None, 1 - core), ("sib", half, first, second))

    return begin, rounds, from_sibling


def pad_matrix(ref, padded_axis):
    chunk = 128
    for start in range(0, ref.shape[0], chunk):
        shape = (chunk, ref.shape[1])
        ids = [lax.broadcasted_iota(jnp.int32, shape, axis) for axis in (0, 1)]
        ids[0] = ids[0] + start
        plain, number = ids[1 - padded_axis], ids[padded_axis]
        block, inner = number // PAD, number % PAD
        hit = jnp.logical_and(inner < ROWS, block * ROWS + inner == plain)
        ref[pl.ds(start, chunk), :] = jnp.where(hit, 1.0, 0.0).astype(BF16)


def rms(inputs):
    widened = inputs.astype(F32)
    return widened, lax.rsqrt(jnp.mean(widened * widened, axis=-1, keepdims=True) + norm_eps)


def back_kernel(
    own_ref, x_ref, cot_ref, gain_ref, scale_ref, down_ref,
    outgoing, rail_ref,
    weights, turned, down_raw, down_turned, spread, gather, normed_pad, wide_pad, inv_ref, gain_pad,
    slope_gate, slope_up, slope_sum, partial, upstream, grads, sides,
    send_sem, recv_sem, wave_send, wave_recv, local_sem,
):
    y, x, core = coords()
    section = lax.axis_index("section")
    sections = lax.axis_size("section")
    last = sections - 1
    tokens, features = x_ref.shape
    hidden = down_ref.shape[0]
    padded = gather.shape[0]
    rail = padded // CORES
    width = padded // RING
    copies = Copies(send_sem, recv_sem)
    fetch = pltpu.make_async_copy(down_ref, down_raw, local_sem)
    fetch.start()
    mine = pl.multiple_of(lax.axis_index("dp") * PAD, PAD)
    weights[pl.ds(mine, PAD), :] = own_ref[...]
    plane_barrier(((section + 1) % sections, (section + sections - 1) % sections))
    begin, rounds, from_sibling = gather_steps(weights, copies, hidden)
    begin(0)
    begin(1)

    pad_matrix(spread, 1)
    one_hot = spread[...]
    widened, inverse = rms(x_ref[...])
    gain = gain_ref[...]
    normed = (widened * inverse * gain).astype(BF16)
    inv_ref[...] = inverse
    high = gain.astype(BF16)
    rest = gain - high.astype(F32)
    middle = rest.astype(BF16)
    low = (rest - middle.astype(F32)).astype(BF16)
    gain_pad[...] = mm(high, one_hot) + mm(middle, one_hot) + mm(low, one_hot)
    wide_pad[...] = mm(x_ref[...], one_hot)
    normed_pad[...] = mm(normed, one_hot).astype(BF16)

    flat = normed_pad[...].T.reshape(padded // (CORES * PAD), CORES, PAD, tokens)
    even = flat[:, 0].reshape(rail, tokens)
    odd = flat[:, 1].reshape(rail, tokens)
    sides[:, pl.ds(0, tokens)] = jnp.where(core == 0, even, odd)
    sides[:, pl.ds(2 * tokens, tokens)] = jnp.where(core == 0, odd, even)
    other = dp_index(y, x, 1 - core)
    copies.start(
        sides.at[:, pl.ds(2 * tokens, tokens)], sides.at[:, pl.ds(tokens, tokens)], "side", other
    )

    def down_piece(start, size):
        down_turned[:, pl.ds(start, size)] = mm(
            gather[...], down_raw[pl.ds(start, size), :], NT
        ).astype(BF16)

    def weight_rows(half, step):
        for i in range(RING):
            from_sibling(half, *((i, step) if half == 0 else (step, i)))
        rows = pl.ds(pl.multiple_of(((y + step) % RING) * width, width), width)
        target = (slope_gate, slope_up)[half]
        left = normed_pad[:, rows]
        for start, size in tiles(hidden):
            here = weights[rows, pl.ds(half * hidden + start, size)]
            turned[pl.ds(half * hidden + start, size), rows] = here.T
            product = mm(left, here)
            cols = pl.ds(start, size)
            target[:, cols] = product if step == 0 else target[:, cols] + product

    downs = [functools.partial(down_piece, *piece) for piece in tiles(hidden, 256)]

    def run(items):
        for item in items:
            item()
            if downs:
                downs.pop(0)()

    run_plain = lambda items: [item() for item in items]
    run_plain(rounds[0])
    pad_matrix(gather, 0)
    fetch.wait()

    @pl.when(section == last)
    def _():
        upstream[...] = mm(cot_ref[...], one_hot).astype(BF16)

    run(rounds[1])
    run(rounds[2])
    weight_rows(0, 0)
    weight_rows(1, 0)
    run(rounds[3])
    while downs:
        downs.pop(0)()
    run(rounds[4])
    weight_rows(1, 3)
    run(rounds[5])
    weight_rows(1, 1)
    run(rounds[6])
    weight_rows(0, 3)
    weight_rows(0, 1)
    weight_rows(0, 2)
    weight_rows(1, 2)

    parts = []
    for size in PARTS:
        parts.append((sum(PARTS[: len(parts)]), size))

    def slopes(first, count):
        rows = pl.ds(first, count)
        for start, size in tiles(hidden):
            cols = pl.ds(start, size)
            gate = slope_gate[rows, cols] * scale_ref[0, 0]
            up = slope_up[rows, cols] * scale_ref[0, 1]
            sigmoid = 1.0 / (1.0 + jnp.exp(-gate))
            by_gate = up * (sigmoid * (1.0 + gate * (1.0 - sigmoid)))
            by_up = gate * sigmoid
            slope_gate[rows, cols] = by_gate
            slope_up[rows, cols] = by_up
            slope_sum[rows, cols] = by_gate * gate + by_up * up

    slopes(*parts[0])

    @pl.when(section < last)
    def _():
        slopes(parts[1][0], tokens - parts[1][0])

    def wave_copy(part, piece):
        rows, cols = pl.ds(*parts[part]), pl.ds(piece * width, width)
        return pltpu.make_async_remote_copy(
            src_ref=outgoing.at[rows, cols],
            dst_ref=upstream.at[rows, cols],
            send_sem=wave_send.at[part * RING + piece],
            recv_sem=wave_recv.at[part * RING + piece],
            device_id={"section": jnp.maximum(section - 1, 0)},
            device_id_type=pl.DeviceIdType.MESH,
        )

    for part, (first, count) in enumerate(parts):
        rows = pl.ds(first, count)
        if part > 0:

            @pl.when(section == last)
            def _():
                slopes(first, count)

        sums = jnp.zeros((count, 128), F32)
        for piece in range(RING):
            span = pl.ds(piece * width, width)

            @pl.when(section < last)
            def _():
                wave_copy(part, piece).wait_recv()

            left = upstream[rows, span]
            for start, size in tiles(hidden):
                cols = pl.ds(start, size)
                product = mm(left, down_turned[span, cols])
                if piece > 0:
                    product = product + partial[pl.ds(0, count), cols]
                if piece < RING - 1:
                    partial[pl.ds(0, count), cols] = product
                    continue
                grads[rows, cols] = (product * slope_gate[rows, cols]).astype(BF16)
                grads[rows, pl.ds(hidden + start, size)] = (product * slope_up[rows, cols]).astype(BF16)
                product = product * slope_sum[rows, cols]
                for lane in range(0, size, 128):
                    sums = sums + product[:, lane : lane + 128]
        copies.start(grads.at[rows], grads.at[pl.ds(tokens + first, count)], ("grads", part), other)
        inverse = inv_ref[rows, :]
        mean = jnp.sum(sums, axis=-1, keepdims=True) * (inverse * inverse / features)
        for piece in range(RING):
            span = pl.ds(piece * width, width)
            normed_grad = (
                mm(grads[rows, pl.ds(0, hidden)], turned[pl.ds(0, hidden), span]) * scale_ref[0, 0]
                + mm(grads[rows, pl.ds(hidden, hidden)], turned[pl.ds(hidden, hidden), span])
                * scale_ref[0, 1]
            )
            outgoing[rows, span] = (
                upstream[rows, span].astype(F32)
                + inverse * (gain_pad[:, span] * normed_grad)
                - wide_pad[rows, span] * mean
            ).astype(BF16)

            @pl.when(section > 0)
            def _():
                wave_copy(part, piece).start()

    copies.wait_recv(sides.at[:, pl.ds(tokens, tokens)], "side")
    for part, (first, count) in enumerate(parts):
        copies.wait_recv(grads.at[pl.ds(tokens + first, count)], ("grads", part))
    both = sides[:, pl.ds(0, 2 * tokens)]
    for start, size in tiles(2 * hidden):
        cols = pl.ds(start, size)
        rail_ref[:, cols] = mm(both, grads[:, cols]).astype(BF16)

    @pl.when(section > 0)
    def _():
        for part in range(len(parts)):
            for piece in range(RING):
                wave_copy(part, piece).wait_send()

    copies.wait_sends()


def adam_update(master, moment_old, second_old, gradient):
    moment_one = beta_one * moment_old + (1.0 - beta_one) * gradient
    moment_two = beta_two * second_old + (1.0 - beta_two) * gradient * gradient
    unbiased_one = moment_one / (1.0 - beta_one**adam_steps)
    unbiased_two = moment_two / (1.0 - beta_two**adam_steps)
    updated = master - learn_rate * (
        unbiased_one / (jnp.sqrt(unbiased_two) + adam_eps) + decay_rate * master
    )
    return (updated, moment_one, moment_two)


def reduce_steps(rail, near, whole, near_last, whole_last, copies, hidden):
    y, x, core = coords()

    def place(half, bulk, other):
        if half == 0:
            return (y + bulk) % RING, (x + other) % RING
        return (y + other) % RING, (x + bulk) % RING

    def block(half, bulk, other, which=None):
        py, px = place(half, bulk, other)
        start, size = {None: (0, PAD), 0: (0, PAD // 2), 1: (PAD // 2, PAD // 2)}[which]
        start = pl.multiple_of((py * RING + px) * PAD + start, PAD // 2)
        return rail.at[pl.ds(start, size), pl.ds(half * hidden, hidden)]

    def send(src, dst, key, half, axis, step):
        py, px = place(half, step, 0) if axis == 0 else place(half, 0, step)
        copies.start(src, dst, key, dp_index(py, px, core))

    def far(half, other):
        for which, step in ((0, 1), (1, -1)):
            send(block(half, 2, other, which), near.at[half, other, which], ("n", half, other, which), half, 0, step)

    def pass_on(half, other):
        for which, step in ((0, 1), (1, -1)):
            copies.wait_recv(near.at[half, other, which], ("n", half, other, which))
            ref = block(half, step, other, which)
            ref[...] = (ref[...].astype(F32) + near[half, other, which].astype(F32)).astype(BF16)
            send(block(half, step, other), whole.at[half, other, which], ("w", half, other, which), half, 0, step)

    def settle(half, other):
        for which in (0, 1):
            copies.wait_recv(whole.at[half, other, which], ("w", half, other, which))
        ref = block(half, 0, other)
        ref[...] = (
            ref[...].astype(F32) + whole[half, other, 0].astype(F32) + whole[half, other, 1].astype(F32)
        ).astype(BF16)

    def far_last(half):
        for which, step in ((0, 1), (1, -1)):
            send(block(half, 0, 2, which), near_last.at[half, which], ("nl", half, which), half, 1, step)

    def pass_last(half):
        for which, step in ((0, 1), (1, -1)):
            copies.wait_recv(near_last.at[half, which], ("nl", half, which))
            ref = block(half, 0, step, which)
            ref[...] = (ref[...].astype(F32) + near_last[half, which].astype(F32)).astype(BF16)
            send(block(half, 0, step), whole_last.at[half, which], ("wl", half, which), half, 1, step)

    def total(half):
        for which in (0, 1):
            copies.wait_recv(whole_last.at[half, which], ("wl", half, which))
        return (
            block(half, 0, 0)[...].astype(F32)
            + whole_last[half, 0].astype(F32)
            + whole_last[half, 1].astype(F32)
        )

    return far, pass_on, settle, far_last, pass_last, total


def update_kernel(
    rail_ref, back_ref, next_ref, gain_ref, mg_ref, mu_ref, og_ref, ou_ref, sg_ref, su_ref,
    result_ref, out_ref, nmg_ref, nmu_ref, nog_ref, nou_ref, nsg_ref, nsu_ref, scale_ref,
    weights, rail, near, whole, near_last, whole_last, spread, gather, next_pad, block_ref, flat_ref,
    state, updates, send_sem, recv_sem, local_sem, state_sem,
):
    y, x, core = coords()
    hidden = out_ref.shape[1]
    features = next_ref.shape[1]
    copies = Copies(send_sem, recv_sem)
    fetch = pltpu.make_async_copy(rail_ref, rail, local_sem)
    fetch.start()
    loads = [
        pltpu.make_async_copy(ref.at[:, 0, :], state.at[i], state_sem.at[i])
        for i, ref in enumerate((mg_ref, mu_ref, og_ref, ou_ref, sg_ref, su_ref))
    ]
    for load in loads:
        load.start()
    plane_barrier()
    fetch.wait()
    far, pass_on, settle, far_last, pass_last, total = reduce_steps(
        rail, near, whole, near_last, whole_last, copies, hidden
    )
    order = (2, 1, 3, 0)
    for other in order:
        far(0, other)
        far(1, other)
    pad_matrix(spread, 1)
    widened, inverse = rms(next_ref[...])
    next_normed = (widened * inverse * gain_ref[...]).astype(BF16)
    next_pad[...] = mm(next_normed, spread[...]).astype(BF16)
    pad_matrix(gather, 0)
    result_ref[...] = mm(back_ref[...], gather[...]).astype(BF16)
    for other in order:
        pass_on(0, other)
        pass_on(1, other)
    for other in order:
        settle(0, other)
        settle(1, other)
        if other == 2:
            far_last(0)
            far_last(1)
    pass_last(0)
    pass_last(1)

    begin, rounds, from_sibling = gather_steps(weights, copies, hidden)
    lanes = flat_ref.shape[1]
    lines = hidden // lanes
    mine = pl.multiple_of(lax.axis_index("dp") * PAD, PAD)
    for load in loads:
        load.wait()
    stores = []
    for half, outs in ((0, (nmg_ref, nog_ref, nsg_ref)), (1, (nmu_ref, nou_ref, nsu_ref))):
        gradient = total(half)
        for line in range(lines):
            flat_ref[pl.ds(line, ROWS, stride=lines), :] = gradient[:ROWS, line * lanes : (line + 1) * lanes]
        gradient = flat_ref[...]
        results = adam_update(state[half], state[2 + half], state[4 + half], gradient)
        for i, value in enumerate(results):
            number = 2 * i + half
            updates[number] = value
            stores.append(
                pltpu.make_async_copy(updates.at[number], outs[i].at[:, 0, :], state_sem.at[number])
            )
            stores[-1].start()
        updated = results[0]
        peak = jnp.max(jnp.abs(updated), keepdims=True)
        high = peak.astype(BF16).astype(F32)
        middle = (peak - high).astype(BF16).astype(F32)
        low = peak - high - middle
        tail = lax.broadcasted_iota(jnp.int32, (PAD - ROWS, hidden), 0)
        for line in range(lines):
            block_ref[pl.ds(0, ROWS), pl.ds(line * lanes, lanes)] = updates[half, pl.ds(line, ROWS, stride=lines), :]
        block_ref[pl.ds(ROWS, PAD - ROWS), :] = jnp.where(
            tail == 0, high, jnp.where(tail == 1, middle, jnp.where(tail == 2, low, 0.0))
        )
        weights[pl.ds(mine, PAD), pl.ds(half * hidden, hidden)] = block_ref[...].astype(BF16)
        begin(half)
    for group in rounds:
        for step in group:
            step()
    for first in range(RING):
        for second in range(RING):
            from_sibling(0, first, second)
            from_sibling(1, first, second)

    peaks = []
    for half in (0, 1):
        heads = weights[:, pl.ds(half * hidden, 128)].astype(F32)
        heads = heads.reshape(heads.shape[0] // PAD, PAD, 128)[:, PAD - 8 :, :]
        level = lax.broadcasted_iota(jnp.int32, heads.shape, 1)
        found = jnp.sum(jnp.where(level >= 4, heads, 0.0), axis=1)
        peaks.append(jnp.max(found, keepdims=True) + scale_eps)
    lane = lax.broadcasted_iota(jnp.int32, scale_ref.shape, 1)
    scale_ref[...] = jnp.where(lane == 0, peaks[0], peaks[1])
    for start, size in tiles(hidden):
        cols = pl.ds(start, size)
        gate = mm(next_pad[...], weights[:, cols])
        up = mm(next_pad[...], weights[:, pl.ds(hidden + start, size)])
        out_ref[:, cols] = (gate / (1.0 + jnp.exp(-gate)) * up).astype(BF16)
    for store in stores:
        store.wait()
    copies.wait_sends()


VMEM = pl.BlockSpec(memory_space=pltpu.VMEM)
SMEM = pl.BlockSpec(memory_space=pltpu.SMEM)
ANY = pl.BlockSpec(memory_space=pl.ANY)


def shards(
    section_inputs,
    cotangent,
    norm_gain,
    quant_gate,
    quant_up,
    scales,
    down_proj,
    master_gate,
    master_up,
    moment_gate,
    moment_up,
    second_gate,
    second_up,
    next_inputs,
):
    tokens, features = cotangent.shape
    hidden = quant_gate.shape[2]
    partners = lax.axis_size("dp")
    padded = partners * PAD
    rail_rows = padded // CORES
    own = jnp.pad(
        jnp.concatenate([quant_gate[0], quant_up[0]], axis=1), ((0, PAD - ROWS), (0, 0))
    )
    dma = pltpu.SemaphoreType.DMA
    back, rail = pl.pallas_call(
        back_kernel,
        out_shape=(
            jax.ShapeDtypeStruct((tokens, padded), BF16),
            jax.ShapeDtypeStruct((rail_rows, 2 * hidden), BF16),
        ),
        in_specs=[VMEM, VMEM, VMEM, VMEM, SMEM, ANY],
        out_specs=(VMEM, VMEM),
        scratch_shapes=[
            pltpu.VMEM((padded, 2 * hidden), BF16),
            pltpu.VMEM((2 * hidden, padded), BF16),
            pltpu.VMEM((hidden, features), BF16),
            pltpu.VMEM((padded, hidden), BF16),
            pltpu.VMEM((features, padded), BF16),
            pltpu.VMEM((padded, features), BF16),
            pltpu.VMEM((tokens, padded), BF16),
            pltpu.VMEM((tokens, padded), F32),
            pltpu.VMEM((tokens, 1), F32),
            pltpu.VMEM((1, padded), F32),
            pltpu.VMEM((tokens, hidden), F32),
            pltpu.VMEM((tokens, hidden), F32),
            pltpu.VMEM((tokens, hidden), F32),
            pltpu.VMEM((max(PARTS), hidden), F32),
            pltpu.VMEM((tokens, padded), BF16),
            pltpu.VMEM((2 * tokens, 2 * hidden), BF16),
            pltpu.VMEM((rail_rows, 3 * tokens), BF16),
            dma((80,)),
            dma((80,)),
            dma((len(PARTS) * RING,)),
            dma((len(PARTS) * RING,)),
            dma(()),
        ],
        compiler_params=pltpu.CompilerParams(
            collective_id=0, has_side_effects=True, vmem_limit_bytes=60 * 2**20
        ),
    )(own, section_inputs[0], cotangent, norm_gain, scales, down_proj[0])
    lanes = 128
    lines = ROWS * hidden // lanes
    row = jax.ShapeDtypeStruct((lines, 1, lanes), F32)
    flat = [
        value.transpose(1, 0, 2).reshape(row.shape)
        for value in (master_gate, master_up, moment_gate, moment_up, second_gate, second_up)
    ]
    outs = pl.pallas_call(
        update_kernel,
        out_shape=(
            jax.ShapeDtypeStruct((tokens, features), BF16),
            jax.ShapeDtypeStruct((tokens, hidden), BF16),
        )
        + (row,) * 6
        + (jax.ShapeDtypeStruct((1, 2), F32),),
        in_specs=[ANY] + [VMEM] * 3 + [ANY] * 6,
        out_specs=(VMEM,) * 2 + (ANY,) * 6 + (VMEM,),
        scratch_shapes=[
            pltpu.VMEM((padded, 2 * hidden), BF16),
            pltpu.VMEM((rail_rows, 2 * hidden), BF16),
            pltpu.VMEM((2, RING, 2, PAD // 2, hidden), BF16),
            pltpu.VMEM((2, RING, 2, PAD, hidden), BF16),
            pltpu.VMEM((2, 2, PAD // 2, hidden), BF16),
            pltpu.VMEM((2, 2, PAD, hidden), BF16),
            pltpu.VMEM((features, padded), BF16),
            pltpu.VMEM((padded, features), BF16),
            pltpu.VMEM((tokens, padded), BF16),
            pltpu.VMEM((PAD, hidden), F32),
            pltpu.VMEM((lines, lanes), F32),
            pltpu.VMEM((6, lines, lanes), F32),
            pltpu.VMEM((6, lines, lanes), F32),
            dma((128,)),
            dma((128,)),
            dma(()),
            dma((6,)),
        ],
        compiler_params=pltpu.CompilerParams(
            collective_id=1, has_side_effects=True, vmem_limit_bytes=60 * 2**20
        ),
    )(rail, back, next_inputs[0], norm_gain, *flat)
    result, next_hidden = outs[:2]
    return (
        (result[None],)
        + tuple(value.reshape(ROWS, 1, hidden).transpose(1, 0, 2) for value in outs[2:8])
        + (outs[8], next_hidden[None])
    )


def solution(mesh):
    placed = (
        P("section", "dp", None),
        P("dp", None),
        P("section", None),
        P("section", "dp", None),
        P("section", "dp", None),
        P("section", None),
        P("section", None, None),
        P("section", "dp", None),
        P("section", "dp", None),
        P("section", "dp", None),
        P("section", "dp", None),
        P("section", "dp", None),
        P("section", "dp", None),
        P("section", "dp", None),
    )
    return jax.shard_map(
        shards,
        mesh=mesh,
        in_specs=placed,
        out_specs=(
            P("section", "dp", None),
            P("section", "dp", None),
            P("section", "dp", None),
            P("section", "dp", None),
            P("section", "dp", None),
            P("section", "dp", None),
            P("section", "dp", None),
            P("section", None),
            P("section", "dp", None),
        ),
        check_vma=False,
    )
```

profile of v0, /device:TPU:1, one launch (start us, length us, event | category | flops | bytes accessed | tf_op | source)
XLA Modules:
  0.0 204.9 jit_solution(15143224796339887245)
XLA Ops:
  0.6 1.7 fusion.2.own_ref
  2.4 115.3 %shard_map.205 = (bf16[256,1024]{1,0:T(8,128)(2,1)}, bf16[512,4864]{1,0:T(8,128)(2,1)}) custom-call(bf16[32,4864]{1,0:T(8,128)(2,1)} %fusion.2.own_ref, bf16[256,896]{1,0:T(8,128)(2,1)} %bitcast.21, bf16[256,896]{1,0:T(8,128)(2,1)} %cot_ref.1, f32[1,896]{1,0:T(1,128)} %gain_ref.3, f32[1,2]{1,0:T(1,128)} %scale_ref.1, bf16[2432,896]{1,0:T(8,128)(2,1)} %bitcast.19), custom_call_target="tpu_custom_call" | custom-call | tf_op jit(solution)/shard_map/pallas_call | solution.py:604
  117.7 72.9 %shard_map.206 = (bf16[256,896]{1,0:T(8,128)(2,1)}, bf16[256,2432]{1,0:T(8,128)(2,1)}, f32[532,1,128]{2,1,0:T(1,128)}, f32[532,1,128]{2,1,0:T(1,128)}, f32[532,1...) custom-call(bf16[512,4864]{1,0:T(8,128)(2,1)} %get-tuple-element.20., ...), custom_call_target="tpu_custom_call" | custom-call | tf_op jit(solution)/shard_map/pallas_call | solution.py:647
  190.6 0.0 copy-start
  190.6 1.9 copy.44
  192.5 1.7 copy.45
  194.2 1.7 copy.46
  195.9 1.7 copy.47
  197.6 1.7 copy.48
  199.3 1.7 copy.49
  201.0 1.7 copy.50
  202.7 1.2 copy.51
  203.9 0.0 copy-done
  203.9 1.0 copy.52
Async XLA Ops:
  190.6 13.3 %copy-start = (bf16[256,2432]{1,0:T(8,128)(2,1)S(1)}, bf16[256,2432]{1,0:T(8,128)(2,1)}, u32[]{:S(2)}) copy-start(bf16[256,2432]{1,0:T(8,128)(2,1)} %get-tuple-element.30) | copy-start | bytes 3735556
where the time goes:
time: 205 us
  Pallas kernels  188 us (92%)
  local copies, waits for them, and re-layouts  14.3 us (7%)
    pallas_call x1, Pallas kernels, shards(): pl.pallas_call(back_kernel, out_shape=(jax.ShapeDtypeStruct((tokens, padd...  115 us
    pallas_call x1, Pallas kernels, shards(): pl.pallas_call(update_kernel, out_shape=(jax.ShapeDtypeStruct((tokens, fe...  72.9 us
    unnamed x11, local copies, waits for them, and re-layouts  14.3 us

commit v1 on v0

--- a/solution.py
+++ b/solution.py
@@ -129,44 +129,46 @@
         for which in (0, 1) if 2 in (first if second == 0 else second,) else (None,):
             copies.wait_recv(piece(half, first, second, which), ("ag", half, first, second, which))
 
-    def spread(half, first):
+    def bulk(half, first):
         send(half, first, 0, None, 1, 1)
         send(half, first, 0, None, 1, -1)
 
-    def on_first(half, first):
-        arrive(half, first, 0)
-        if first == 3:
-            send(half, first, 0, 0, 0, 1)
-        if first == 1:
-            send(half, first, 0, 1, 0, -1)
-        spread(half, first)
-        sibling(half, first, 0)
-
-    def on_second(half, first, second):
+    def relay(half, first, second):
         arrive(half, first, second)
-        if second == 3:
-            send(half, first, second, 0, 1, 1)
-        if second == 1:
-            send(half, first, second, 1, 1, -1)
-        sibling(half, first, second)
+        axis = 0 if second == 0 else 1
+        if (first, second)[axis] == 3:
+            send(half, first, second, 0, axis, 1)
+        else:
+            send(half, first, second, 1, axis, -1)
 
     def begin(half):
         send(half, 0, 0, None, 0, 1)
         send(half, 0, 0, None, 0, -1)
-        spread(half, 0)
+        bulk(half, 0)
         sibling(half, 0, 0)
 
-    def both(step, *key):
-        return [functools.partial(step, half, *key) for half in (0, 1)]
+    def group(*steps):
+        return [functools.partial(step, half, *key) for step, *key in steps for half in (0, 1)]
+
+    def lines(first, *more):
+        return group(
+            (relay, first, 3), (relay, first, 1), *more, (sibling, first, 3), (sibling, first, 1)
+        )
+
+    def opposite(first, second):
+        return group((arrive, first, second), (sibling, first, second))
 
     rounds = (
-        both(on_first, 3) + both(on_first, 1),
-        both(on_second, 0, 3) + both(on_second, 0, 1) + both(on_first, 2),
-        both(on_second, 0, 2),
-        both(on_second, 3, 3) + both(on_second, 3, 1) + both(on_second, 1, 3) + both(on_second, 1, 1),
-        both(on_second, 3, 2) + both(on_second, 1, 2),
-        both(on_second, 2, 3) + both(on_second, 2, 1),
-        both(on_second, 2, 2),
+        group((relay, 3, 0), (relay, 1, 0), (bulk, 3), (sibling, 3, 0), (sibling, 1, 0)),
+        lines(0, (bulk, 1)),
+        opposite(2, 0),
+        lines(3, (bulk, 2)),
+        opposite(0, 2),
+        lines(1),
+        opposite(3, 2),
+        lines(2),
+        opposite(1, 2),
+        opposite(2, 2),
     )
 
     def from_sibling(half, first, second):
@@ -193,10 +195,10 @@
 
 
 def back_kernel(
-    own_ref, x_ref, cot_ref, gain_ref, scale_ref, down_ref,
+    gate_ref, up_ref, x_ref, cot_ref, gain_ref, scale_ref, down_ref,
     outgoing, rail_ref,
     weights, turned, down_raw, down_turned, spread, gather, normed_pad, wide_pad, inv_ref, gain_pad,
-    slope_gate, slope_up, slope_sum, partial, upstream, grads, sides,
+    slope_gate, slope_up, slope_sum, partial, upstream, grads, sides, block,
     send_sem, recv_sem, wave_send, wave_recv, local_sem,
 ):
     y, x, core = coords()
@@ -212,7 +214,10 @@
     fetch = pltpu.make_async_copy(down_ref, down_raw, local_sem)
     fetch.start()
     mine = pl.multiple_of(lax.axis_index("dp") * PAD, PAD)
-    weights[pl.ds(mine, PAD), :] = own_ref[...]
+    block[...] = jnp.zeros(block.shape, BF16)
+    block[pl.ds(0, ROWS), pl.ds(0, hidden)] = gate_ref[...]
+    block[pl.ds(0, ROWS), pl.ds(hidden, hidden)] = up_ref[...]
+    weights[pl.ds(mine, PAD), :] = block[...]
     plane_barrier(((section + 1) % sections, (section + sections - 1) % sections))
     begin, rounds, from_sibling = gather_steps(weights, copies, hidden)
     begin(0)
@@ -262,14 +267,13 @@
 
     downs = [functools.partial(down_piece, *piece) for piece in tiles(hidden, 256)]
 
-    def run(items):
+    def run(items, count=0):
         for item in items:
             item()
-            if downs:
-                downs.pop(0)()
-
-    run_plain = lambda items: [item() for item in items]
-    run_plain(rounds[0])
+        for _ in range(count):
+            downs.pop(0)()
+
+    run(rounds[0])
     pad_matrix(gather, 0)
     fetch.wait()
 
@@ -277,18 +281,19 @@
     def _():
         upstream[...] = mm(cot_ref[...], one_hot).astype(BF16)
 
-    run(rounds[1])
+    run(rounds[1], 2)
     run(rounds[2])
     weight_rows(0, 0)
+    run(rounds[3], 3)
+    run(rounds[4])
     weight_rows(1, 0)
-    run(rounds[3])
-    while downs:
-        downs.pop(0)()
-    run(rounds[4])
+    run(rounds[5], 3)
+    run(rounds[6])
     weight_rows(1, 3)
-    run(rounds[5])
+    run(rounds[7], len(downs))
+    run(rounds[8])
     weight_rows(1, 1)
-    run(rounds[6])
+    run(rounds[9])
     weight_rows(0, 3)
     weight_rows(0, 1)
     weight_rows(0, 2)
@@ -470,7 +475,7 @@
     rail_ref, back_ref, next_ref, gain_ref, mg_ref, mu_ref, og_ref, ou_ref, sg_ref, su_ref,
     result_ref, out_ref, nmg_ref, nmu_ref, nog_ref, nou_ref, nsg_ref, nsu_ref, scale_ref,
     weights, rail, near, whole, near_last, whole_last, spread, gather, next_pad, block_ref, flat_ref,
-    state, updates, send_sem, recv_sem, local_sem, state_sem,
+    state, updates, gate_sum, up_sum, send_sem, recv_sem, local_sem, state_sem,
 ):
     y, x, core = coords()
     hidden = out_ref.shape[1]
@@ -544,13 +549,37 @@
         )
         weights[pl.ds(mine, PAD), pl.ds(half * hidden, hidden)] = block_ref[...].astype(BF16)
         begin(half)
-    for group in rounds:
-        for step in group:
-            step()
-    for first in range(RING):
-        for second in range(RING):
-            from_sibling(0, first, second)
-            from_sibling(1, first, second)
+    width = next_pad.shape[1] // RING
+
+    def line_of(half, step, cols):
+        rows = pl.ds(pl.multiple_of(((y + step) % RING) * width, width), width)
+        return mm(next_pad[:, rows], weights[rows, pl.ds(half * hidden + cols.start, cols.size)])
+
+    def line_ready(half, step):
+        for i in range(RING):
+            from_sibling(half, *((i, step) if half == 0 else (step, i)))
+
+    def add_line(half, step, target, fresh):
+        line_ready(half, step)
+        for piece in tiles(hidden):
+            cols = pl.ds(*piece)
+            product = line_of(half, step, cols)
+            target[:, cols] = product if fresh else target[:, cols] + product
+
+    after = {
+        2: lambda: add_line(0, 0, gate_sum, True),
+        4: lambda: add_line(1, 0, up_sum, True),
+        6: lambda: add_line(1, 3, up_sum, False),
+        8: lambda: add_line(1, 1, up_sum, False),
+    }
+    for number, items in enumerate(rounds):
+        for item in items:
+            item()
+        if number in after:
+            after[number]()
+    for step in (3, 1, 2):
+        line_ready(0, step)
+    line_ready(1, 2)
 
     peaks = []
     for half in (0, 1):
@@ -563,17 +592,43 @@
     scale_ref[...] = jnp.where(lane == 0, peaks[0], peaks[1])
     for start, size in tiles(hidden):
         cols = pl.ds(start, size)
-        gate = mm(next_pad[...], weights[:, cols])
-        up = mm(next_pad[...], weights[:, pl.ds(hidden + start, size)])
+        gate = gate_sum[:, cols]
+        for step in (3, 1, 2):
+            gate = gate + line_of(0, step, cols)
+        up = up_sum[:, cols] + line_of(1, 2, cols)
         out_ref[:, cols] = (gate / (1.0 + jnp.exp(-gate)) * up).astype(BF16)
     for store in stores:
         store.wait()
     copies.wait_sends()
 
 
+def deliver_kernel(count, *refs):
+    sources, targets = refs[:count], refs[count : 2 * count]
+    holds, load_sem, store_sem = refs[2 * count : 3 * count - 1], refs[-2], refs[-1]
+
+    def flat(ref):
+        return ref.at[:, 0, :] if len(ref.shape) == 3 else ref
+
+    loads = [
+        pltpu.make_async_copy(flat(sources[i]), hold, load_sem.at[i]) for i, hold in enumerate(holds)
+    ]
+    stores = [
+        pltpu.make_async_copy(hold, flat(targets[i]), store_sem.at[i]) for i, hold in enumerate(holds)
+    ]
+    for load in loads:
+        load.start()
+    targets[-1][...] = sources[-1][...]
+    for load, store in zip(loads, stores):
+        load.wait()
+        store.start()
+    for store in stores:
+        store.wait()
+
+
 VMEM = pl.BlockSpec(memory_space=pltpu.VMEM)
 SMEM = pl.BlockSpec(memory_space=pltpu.SMEM)
 ANY = pl.BlockSpec(memory_space=pl.ANY)
+HBM = pl.BlockSpec(memory_space=pltpu.HBM)
 
 
 def shards(
@@ -597,9 +652,6 @@
     partners = lax.axis_size("dp")
     padded = partners * PAD
     rail_rows = padded // CORES
-    own = jnp.pad(
-        jnp.concatenate([quant_gate[0], quant_up[0]], axis=1), ((0, PAD - ROWS), (0, 0))
-    )
     dma = pltpu.SemaphoreType.DMA
     back, rail = pl.pallas_call(
         back_kernel,
@@ -607,7 +659,7 @@
             jax.ShapeDtypeStruct((tokens, padded), BF16),
             jax.ShapeDtypeStruct((rail_rows, 2 * hidden), BF16),
         ),
-        in_specs=[VMEM, VMEM, VMEM, VMEM, SMEM, ANY],
+        in_specs=[VMEM, VMEM, VMEM, VMEM, VMEM, SMEM, ANY],
         out_specs=(VMEM, VMEM),
         scratch_shapes=[
             pltpu.VMEM((padded, 2 * hidden), BF16),
@@ -627,6 +679,7 @@
             pltpu.VMEM((tokens, padded), BF16),
             pltpu.VMEM((2 * tokens, 2 * hidden), BF16),
             pltpu.VMEM((rail_rows, 3 * tokens), BF16),
+            pltpu.VMEM((PAD, 2 * hidden), BF16),
             dma((80,)),
             dma((80,)),
             dma((len(PARTS) * RING,)),
@@ -636,7 +689,7 @@
         compiler_params=pltpu.CompilerParams(
             collective_id=0, has_side_effects=True, vmem_limit_bytes=60 * 2**20
         ),
-    )(own, section_inputs[0], cotangent, norm_gain, scales, down_proj[0])
+    )(quant_gate[0], quant_up[0], section_inputs[0], cotangent, norm_gain, scales, down_proj[0])
     lanes = 128
     lines = ROWS * hidden // lanes
     row = jax.ShapeDtypeStruct((lines, 1, lanes), F32)
@@ -668,6 +721,8 @@
             pltpu.VMEM((lines, lanes), F32),
             pltpu.VMEM((6, lines, lanes), F32),
             pltpu.VMEM((6, lines, lanes), F32),
+            pltpu.VMEM((tokens, hidden), F32),
+            pltpu.VMEM((tokens, hidden), F32),
             dma((128,)),
             dma((128,)),
             dma(()),
@@ -677,6 +732,17 @@
             collective_id=1, has_side_effects=True, vmem_limit_bytes=60 * 2**20
         ),
     )(rail, back, next_inputs[0], norm_gain, *flat)
+    outs = pl.pallas_call(
+        functools.partial(deliver_kernel, len(outs)),
+        out_shape=tuple(jax.ShapeDtypeStruct(value.shape, value.dtype) for value in outs),
+        in_specs=[HBM] * 8 + [VMEM],
+        out_specs=(HBM,) * 8 + (VMEM,),
+        scratch_shapes=[
+            pltpu.VMEM((value.shape[0], value.shape[-1]), value.dtype) for value in outs[:-1]
+        ]
+        + [dma((8,)), dma((8,))],
+        compiler_params=pltpu.CompilerParams(vmem_limit_bytes=60 * 2**20),
+    )(*outs)
     result, next_hidden = outs[:2]
     return (
         (result[None],)

time: 205 us -> 183 us (0.89)
  local copies, waits for them, and re-layouts: 14.3 us -> 0 us
  Pallas kernels: 188 us -> 182 us
    unnamed x11 -> x0, local copies, waits for them, and re-layouts: 14.3 us -> none
    pallas_call x1, Pallas kernels: 115 us -> 110 us  [shards(): pl.pallas_call(back_kernel, out_shape=(jax.ShapeDtypeStruct((tokens, padd...]
    pallas_call x1, Pallas kernels: 72.9 us -> 68.3 us  [shards(): pl.pallas_call(update_kernel, out_shape=(jax.ShapeDtypeStruct((tokens, fe...]
    pallas_call x0 -> x1, Pallas kernels: none -> 4.31 us  [shards(): pl.pallas_call(functools.partial(deliver_kernel, len(outs)), out_shape=tu...]
where the time goes in v1:
time: 183 us
  Pallas kernels  182 us (99%)
    pallas_call x1, Pallas kernels, shards(): pl.pallas_call(back_kernel, out_shape=(jax.ShapeDtypeStruct((tokens, padd...  110 us
    pallas_call x1, Pallas kernels, shards(): pl.pallas_call(update_kernel, out_shape=(jax.ShapeDtypeStruct((tokens, fe...  68.3 us
    pallas_call x1, Pallas kernels, shards(): pl.pallas_call(functools.partial(deliver_kernel, len(outs)), out_shape=tu...  4.31 us

profile of v1, /device:TPU:1, one launch (start us, length us, event | category | flops | bytes accessed | tf_op | source)
XLA Modules:
  0.0 183.3 jit_solution(2430111910739462730)
XLA Ops:
  0.6 109.8 %shard_map.205 = (bf16[256,1024]{1,0:T(8,128)(2,1)}, bf16[512,4864]{1,0:T(8,128)(2,1)}) custom-call(bf16[28,2432]{1,0:T(8,128)(2,1)} %bitcast.28, bf16[28,2432]{1,0:T(8,128)(2,1)} %bitcast.29, bf16[256,896]{1,0:T(8,128)(2,1)} %bitcast.20, bf16[256,896]{1,0:T(8,128)(2,1)} %cot_ref.1, f32[1,896]{1,0:T(1,128)} %gain_ref.3, f32[1,2]{1,0:T(1,128)} %scale_ref.1, ...), custom_call_target="tpu_custom_call" | custom-call | tf_op jit(solution)/shard_map/pallas_call | solution.py:656
  110.5 68.3 %shard_map.206 = (bf16[256,896]{1,0:T(8,128)(2,1)}, bf16[256,2432]{1,0:T(8,128)(2,1)}, f32[532,1,128]{2,1,0:T(1,128)}, f32[532,1,128]{2,1,0:T(1,128)}, f32[532,1...) custom-call(bf16[512,4864]{1,0:T(8,128)(2,1)} %get-tuple-element.29., ...), custom_call_target="tpu_custom_call" | custom-call | tf_op jit(solution)/shard_map/pallas_call | solution.py:700
  178.7 4.3 %shard_map.207 = (bf16[256,896]{1,0:T(8,128)(2,1)}, bf16[256,2432]{1,0:T(8,128)(2,1)}, f32[532,1,128]{2,1,0:T(1,128)}, f32[532,1,128]{2,1,0:T(1,128)}, f32[532,1...) custom-call(bf16[256,896]{1,0:T(8,128)(2,1)} %get-tuple-element.31.r, ...), custom_call_target="tpu_custom_call" | custom-call | tf_op jit(solution)/shard_map/pallas_call | solution.py:735

commit v2 on v1

--- a/solution.py
+++ b/solution.py
@@ -19,6 +19,7 @@
 CORES = 2
 ROWS = 28
 PAD = 32
+KEEP = 1920
 PARTS = (64, 64, 64, 64)
 F32 = jnp.float32
 BF16 = jnp.bfloat16
@@ -96,6 +97,38 @@
     pl.semaphore_wait(sem, 5 + len(extra))
 
 
+def part_of(ref, row, col, which, hidden):
+    row = pl.multiple_of(row + which * (PAD // 2), PAD // 2)
+    return ref.at[pl.ds(row, PAD // 2), pl.ds(col, KEEP if which else hidden)]
+
+
+def pack(ref, row, col, hidden):
+    extra = hidden - KEEP
+    rows = pl.ds(pl.multiple_of(row + PAD // 2, PAD // 2), PAD // 2)
+    source = ref[rows, pl.ds(col + KEEP, extra)].astype(F32)
+    number = lax.broadcasted_iota(jnp.int32, source.shape, 0)
+    for i in range(3):
+        cols = pl.ds(col + i * extra, extra)
+        moved = pltpu.roll(source, 12 - 4 * i, 0)
+        ref[rows, cols] = jnp.where(number >= 12, moved, ref[rows, cols].astype(F32)).astype(ref.dtype)
+
+
+def last_columns(lower, extra):
+    number = lax.broadcasted_iota(jnp.int32, (lower.shape[0], extra), 0)
+    result = jnp.zeros((lower.shape[0], extra), F32)
+    for i in range(3):
+        moved = pltpu.roll(lower[:, i * extra : (i + 1) * extra], 4 + 4 * i, 0)
+        result = jnp.where(number // 4 == i, moved, result)
+    return result
+
+
+def unpack(ref, row, col, hidden):
+    extra = hidden - KEEP
+    rows = pl.ds(pl.multiple_of(row + PAD // 2, PAD // 2), PAD // 2)
+    lower = ref[rows, pl.ds(col, 3 * extra)].astype(F32)
+    ref[rows, pl.ds(col + KEEP, extra)] = last_columns(lower, extra).astype(BF16)
+
+
 def gather_steps(buf, copies, hidden):
     y, x, core = coords()
 
@@ -107,9 +140,7 @@
     def piece(half, first, second, which, owner_core=None):
         py, px = place(half, first, second)
         base = dp_index(py, px, core if owner_core is None else owner_core) * PAD
-        start, size = {None: (0, PAD), 0: (0, PAD // 2), 1: (PAD // 2, PAD // 2)}[which]
-        start = pl.multiple_of(base + start, PAD // 2)
-        return buf.at[pl.ds(start, size), pl.ds(half * hidden, hidden)]
+        return part_of(buf, base, half * hidden, which, hidden)
 
     def send(half, first, second, which, axis, step):
         if axis == 0:
@@ -122,28 +153,37 @@
         copies.start(ref, ref, key, dp_index(py, px, core))
 
     def sibling(half, first, second):
-        ref = piece(half, first, second, None)
-        copies.start(ref, ref, ("sib", half, first, second), dp_index(y, x, 1 - core))
+        for which in (0, 1):
+            ref = piece(half, first, second, which)
+            copies.start(ref, ref, ("sib", half, first, second, which), dp_index(y, x, 1 - core))
+
+    def landed(half, first, second, which):
+        copies.wait_recv(piece(half, first, second, which), ("ag", half, first, second, which))
 
     def arrive(half, first, second):
-        for which in (0, 1) if 2 in (first if second == 0 else second,) else (None,):
-            copies.wait_recv(piece(half, first, second, which), ("ag", half, first, second, which))
+        landed(half, first, second, 0)
+        landed(half, first, second, 1)
+
+    def both_ways(half, first, axis):
+        for which in (0, 1):
+            send(half, first, 0, which, axis, 1)
+            send(half, first, 0, which, axis, -1)
 
     def bulk(half, first):
-        send(half, first, 0, None, 1, 1)
-        send(half, first, 0, None, 1, -1)
+        both_ways(half, first, 1)
 
     def relay(half, first, second):
-        arrive(half, first, second)
         axis = 0 if second == 0 else 1
-        if (first, second)[axis] == 3:
-            send(half, first, second, 0, axis, 1)
-        else:
-            send(half, first, second, 1, axis, -1)
+        step = 1 if (first, second)[axis] == 3 else -1
+        which = 0 if step == 1 else 1
+        if axis == 1 and first in (1, 2):
+            which = 1 - which
+        landed(half, first, second, which)
+        send(half, first, second, which, axis, step)
+        landed(half, first, second, 1 - which)
 
     def begin(half):
-        send(half, 0, 0, None, 0, 1)
-        send(half, 0, 0, None, 0, -1)
+        both_ways(half, 0, 0)
         bulk(half, 0)
         sibling(half, 0, 0)
 
@@ -172,7 +212,10 @@
     )
 
     def from_sibling(half, first, second):
-        copies.wait_recv(piece(half, first, second, None, 1 - core), ("sib", half, first, second))
+        for which in (0, 1):
+            copies.wait_recv(
+                piece(half, first, second, which, 1 - core), ("sib", half, first, second, which)
+            )
 
     return begin, rounds, from_sibling
 
@@ -217,6 +260,8 @@
     block[...] = jnp.zeros(block.shape, BF16)
     block[pl.ds(0, ROWS), pl.ds(0, hidden)] = gate_ref[...]
     block[pl.ds(0, ROWS), pl.ds(hidden, hidden)] = up_ref[...]
+    pack(block, 0, 0, hidden)
+    pack(block, 0, hidden, hidden)
     weights[pl.ds(mine, PAD), :] = block[...]
     plane_barrier(((section + 1) % sections, (section + sections - 1) % sections))
     begin, rounds, from_sibling = gather_steps(weights, copies, hidden)
@@ -256,6 +301,8 @@
         for i in range(RING):
             from_sibling(half, *((i, step) if half == 0 else (step, i)))
         rows = pl.ds(pl.multiple_of(((y + step) % RING) * width, width), width)
+        for number in range(width // PAD):
+            unpack(weights, ((y + step) % RING) * width + number * PAD, half * hidden, hidden)
         target = (slope_gate, slope_up)[half]
         left = normed_pad[:, rows]
         for start, size in tiles(hidden):
@@ -419,54 +466,71 @@
             return (y + bulk) % RING, (x + other) % RING
         return (y + other) % RING, (x + bulk) % RING
 
-    def block(half, bulk, other, which=None):
+    def block(half, bulk, other, which):
         py, px = place(half, bulk, other)
-        start, size = {None: (0, PAD), 0: (0, PAD // 2), 1: (PAD // 2, PAD // 2)}[which]
-        start = pl.multiple_of((py * RING + px) * PAD + start, PAD // 2)
-        return rail.at[pl.ds(start, size), pl.ds(half * hidden, hidden)]
+        return part_of(rail, (py * RING + px) * PAD, half * hidden, which, hidden)
 
     def send(src, dst, key, half, axis, step):
         py, px = place(half, step, 0) if axis == 0 else place(half, 0, step)
         copies.start(src, dst, key, dp_index(py, px, core))
 
+    def ways(other):
+        return ((0, 1), (1, -1)) if other in (0, 3) else ((1, 1), (0, -1))
+
+    def trim(ref, which):
+        return part_of(ref, 0, 0, which, hidden)
+
+    def narrow(ref, which):
+        return ref.at[:, pl.ds(0, KEEP)] if which else ref
+
     def far(half, other):
-        for which, step in ((0, 1), (1, -1)):
-            send(block(half, 2, other, which), near.at[half, other, which], ("n", half, other, which), half, 0, step)
+        for which, step in ways(other):
+            send(block(half, 2, other, which), narrow(near.at[half, other, which], which), ("n", half, other, which), half, 0, step)
 
     def pass_on(half, other):
-        for which, step in ((0, 1), (1, -1)):
-            copies.wait_recv(near.at[half, other, which], ("n", half, other, which))
+        for which, step in ways(other):
+            here = narrow(near.at[half, other, which], which)
+            copies.wait_recv(here, ("n", half, other, which))
             ref = block(half, step, other, which)
-            ref[...] = (ref[...].astype(F32) + near[half, other, which].astype(F32)).astype(BF16)
-            send(block(half, step, other), whole.at[half, other, which], ("w", half, other, which), half, 0, step)
+            ref[...] = (ref[...].astype(F32) + here[...].astype(F32)).astype(BF16)
+            side = 0 if step == 1 else 1
+            for part in (0, 1):
+                send(block(half, step, other, part), trim(whole.at[half, other, side], part), ("w", half, other, side, part), half, 0, step)
 
     def settle(half, other):
-        for which in (0, 1):
-            copies.wait_recv(whole.at[half, other, which], ("w", half, other, which))
-        ref = block(half, 0, other)
-        ref[...] = (
-            ref[...].astype(F32) + whole[half, other, 0].astype(F32) + whole[half, other, 1].astype(F32)
-        ).astype(BF16)
+        for part in (0, 1):
+            ref = block(half, 0, other, part)
+            value = ref[...].astype(F32)
+            for side in (0, 1):
+                here = trim(whole.at[half, other, side], part)
+                copies.wait_recv(here, ("w", half, other, side, part))
+                value = value + here[...].astype(F32)
+            ref[...] = value.astype(BF16)
 
     def far_last(half):
-        for which, step in ((0, 1), (1, -1)):
-            send(block(half, 0, 2, which), near_last.at[half, which], ("nl", half, which), half, 1, step)
+        for which, step in ways(0):
+            send(block(half, 0, 2, which), narrow(near_last.at[half, which], which), ("nl", half, which), half, 1, step)
 
     def pass_last(half):
-        for which, step in ((0, 1), (1, -1)):
-            copies.wait_recv(near_last.at[half, which], ("nl", half, which))
+        for which, step in ways(0):
+            here = narrow(near_last.at[half, which], which)
+            copies.wait_recv(here, ("nl", half, which))
             ref = block(half, 0, step, which)
-            ref[...] = (ref[...].astype(F32) + near_last[half, which].astype(F32)).astype(BF16)
-            send(block(half, 0, step), whole_last.at[half, which], ("wl", half, which), half, 1, step)
+            ref[...] = (ref[...].astype(F32) + here[...].astype(F32)).astype(BF16)
+            side = 0 if step == 1 else 1
+            for part in (0, 1):
+                send(block(half, 0, step, part), trim(whole_last.at[half, side], part), ("wl", half, side, part), half, 1, step)
 
     def total(half):
-        for which in (0, 1):
-            copies.wait_recv(whole_last.at[half, which], ("wl", half, which))
-        return (
-            block(half, 0, 0)[...].astype(F32)
-            + whole_last[half, 0].astype(F32)
-            + whole_last[half, 1].astype(F32)
-        )
+        sums = []
+        for part in (0, 1):
+            value = block(half, 0, 0, part)[...].astype(F32)
+            for side in (0, 1):
+                here = trim(whole_last.at[half, side], part)
+                copies.wait_recv(here, ("wl", half, side, part))
+                value = value + here[...].astype(F32)
+            sums.append(value)
+        return sums
 
     return far, pass_on, settle, far_last, pass_last, total
 
@@ -491,6 +555,9 @@
         load.start()
     plane_barrier()
     fetch.wait()
+    for number in range(rail.shape[0] // PAD):
+        pack(rail, number * PAD, 0, hidden)
+        pack(rail, number * PAD, hidden, hidden)
     far, pass_on, settle, far_last, pass_last, total = reduce_steps(
         rail, near, whole, near_last, whole_last, copies, hidden
     )
@@ -524,9 +591,14 @@
         load.wait()
     stores = []
     for half, outs in ((0, (nmg_ref, nog_ref, nsg_ref)), (1, (nmu_ref, nou_ref, nsu_ref))):
-        gradient = total(half)
+        upper, lower = total(half)
+        lower = jnp.concatenate([lower, last_columns(lower, hidden - KEEP)], axis=1)
         for line in range(lines):
-            flat_ref[pl.ds(line, ROWS, stride=lines), :] = gradient[:ROWS, line * lanes : (line + 1) * lanes]
+            span = slice(line * lanes, (line + 1) * lanes)
+            flat_ref[pl.ds(line, PAD // 2, stride=lines), :] = upper[:, span]
+            flat_ref[pl.ds(PAD // 2 * lines + line, ROWS - PAD // 2, stride=lines), :] = lower[
+                : ROWS - PAD // 2, span
+            ]
         gradient = flat_ref[...]
         results = adam_update(state[half], state[2 + half], state[4 + half], gradient)
         for i, value in enumerate(results):
@@ -547,6 +619,7 @@
         block_ref[pl.ds(ROWS, PAD - ROWS), :] = jnp.where(
             tail == 0, high, jnp.where(tail == 1, middle, jnp.where(tail == 2, low, 0.0))
         )
+        pack(block_ref, 0, 0, hidden)
         weights[pl.ds(mine, PAD), pl.ds(half * hidden, hidden)] = block_ref[...].astype(BF16)
         begin(half)
     width = next_pad.shape[1] // RING
@@ -558,6 +631,8 @@
     def line_ready(half, step):
         for i in range(RING):
             from_sibling(half, *((i, step) if half == 0 else (step, i)))
+        for number in range(width // PAD):
+            unpack(weights, ((y + step) % RING) * width + number * PAD, half * hidden, hidden)
 
     def add_line(half, step, target, fresh):
         line_ready(half, step)
@@ -583,7 +658,7 @@
 
     peaks = []
     for half in (0, 1):
-        heads = weights[:, pl.ds(half * hidden, 128)].astype(F32)
+        heads = weights[:, pl.ds(half * hidden + 3 * (hidden - KEEP), 128)].astype(F32)
         heads = heads.reshape(heads.shape[0] // PAD, PAD, 128)[:, PAD - 8 :, :]
         level = lax.broadcasted_iota(jnp.int32, heads.shape, 1)
         found = jnp.sum(jnp.where(level >= 4, heads, 0.0), axis=1)
@@ -680,8 +755,8 @@
             pltpu.VMEM((2 * tokens, 2 * hidden), BF16),
             pltpu.VMEM((rail_rows, 3 * tokens), BF16),
             pltpu.VMEM((PAD, 2 * hidden), BF16),
-            dma((80,)),
-            dma((80,)),
+            dma((160,)),
+            dma((160,)),
             dma((len(PARTS) * RING,)),
             dma((len(PARTS) * RING,)),
             dma(()),
@@ -723,8 +798,8 @@
             pltpu.VMEM((6, lines, lanes), F32),
             pltpu.VMEM((tokens, hidden), F32),
             pltpu.VMEM((tokens, hidden), F32),
-            dma((128,)),
-            dma((128,)),
+            dma((200,)),
+            dma((200,)),
             dma(()),
             dma((6,)),
         ],

time: 183 us -> 185 us (1.011); the launches traced: 183 us -> 182 us
    pallas_call x1, Pallas kernels: 68.3 us -> 65.1 us  [shards(): pl.pallas_call(update_kernel, out_shape=(jax.ShapeDtypeStruct((tokens, fe...]
where the time goes in v2:
time: 185 us; the launch traced here: 182 us
  Pallas kernels  181 us (98%)
    pallas_call x1, Pallas kernels, shards(): pl.pallas_call(back_kernel, out_shape=(jax.ShapeDtypeStruct((tokens, padd...  111 us
    pallas_call x1, Pallas kernels, shards(): pl.pallas_call(update_kernel, out_shape=(jax.ShapeDtypeStruct((tokens, fe...  65.1 us
    pallas_call x1, Pallas kernels, shards(): pl.pallas_call(functools.partial(deliver_kernel, len(outs)), out_shape=tu...  4.31 us

profile of v2, /device:TPU:1, one launch (start us, length us, event | category | flops | bytes accessed | tf_op | source)
XLA Modules:
  0.0 181.6 jit_solution(11833243592849909525)
XLA Ops:
  0.6 111.3 %shard_map.205 = (bf16[256,1024]{1,0:T(8,128)(2,1)}, bf16[512,4864]{1,0:T(8,128)(2,1)}) custom-call(bf16[28,2432]{1,0:T(8,128)(2,1)} %bitcast.28, bf16[28,2432]{1,0:T(8,128)(2,1)} %bitcast.29, bf16[256,896]{1,0:T(8,128)(2,1)} %bitcast.20, bf16[256,896]{1,0:T(8,128)(2,1)} %cot_ref.1, f32[1,896]{1,0:T(1,128)} %gain_ref.3, f32[1,2]{1,0:T(1,128)} %scale_ref.1, ...), custom_call_target="tpu_custom_call" | custom-call | tf_op jit(solution)/shard_map/pallas_call | solution.py:731
  111.9 65.1 %shard_map.206 = (bf16[256,896]{1,0:T(8,128)(2,1)}, bf16[256,2432]{1,0:T(8,128)(2,1)}, f32[532,1,128]{2,1,0:T(1,128)}, f32[532,1,128]{2,1,0:T(1,128)}, f32[532,1...) custom-call(bf16[512,4864]{1,0:T(8,128)(2,1)} %get-tuple-element.29., ...), custom_call_target="tpu_custom_call" | custom-call | tf_op jit(solution)/shard_map/pallas_call | solution.py:775
  177.0 4.3 %shard_map.207 = (bf16[256,896]{1,0:T(8,128)(2,1)}, bf16[256,2432]{1,0:T(8,128)(2,1)}, f32[532,1,128]{2,1,0:T(1,128)}, f32[532,1,128]{2,1,0:T(1,128)}, f32[532,1...) custom-call(bf16[256,896]{1,0:T(8,128)(2,1)} %get-tuple-element.31.r, ...), custom_call_target="tpu_custom_call" | custom-call | tf_op jit(solution)/shard_map/pallas_call | solution.py:810

commit v3 on v2

--- a/solution.py
+++ b/solution.py
@@ -241,8 +241,8 @@
     gate_ref, up_ref, x_ref, cot_ref, gain_ref, scale_ref, down_ref,
     outgoing, rail_ref,
     weights, turned, down_raw, down_turned, spread, gather, normed_pad, wide_pad, inv_ref, gain_pad,
-    slope_gate, slope_up, slope_sum, partial, upstream, grads, sides, block,
-    send_sem, recv_sem, wave_send, wave_recv, local_sem,
+    slope_gate, slope_up, slope_sum, partial, upstream, grads, sides, block, rail_hold,
+    send_sem, recv_sem, wave_send, wave_recv, local_sem, rail_sem,
 ):
     y, x, core = coords()
     section = lax.axis_index("section")
@@ -324,9 +324,19 @@
     pad_matrix(gather, 0)
     fetch.wait()
 
+    parts = []
+    for size in PARTS:
+        parts.append((sum(PARTS[: len(parts)]), size))
+
     @pl.when(section == last)
     def _():
-        upstream[...] = mm(cot_ref[...], one_hot).astype(BF16)
+        outgoing[...] = mm(cot_ref[...], one_hot).astype(BF16)
+        for part, place in enumerate(parts):
+            for piece in range(RING):
+                region = (pl.ds(*place), pl.ds(piece * width, width))
+                pltpu.make_async_copy(
+                    outgoing.at[region], upstream.at[region], wave_recv.at[part * RING + piece]
+                ).start()
 
     run(rounds[1], 2)
     run(rounds[2])
@@ -346,10 +356,6 @@
     weight_rows(0, 2)
     weight_rows(1, 2)
 
-    parts = []
-    for size in PARTS:
-        parts.append((sum(PARTS[: len(parts)]), size))
-
     def slopes(first, count):
         rows = pl.ds(first, count)
         for start, size in tiles(hidden):
@@ -391,11 +397,7 @@
         sums = jnp.zeros((count, 128), F32)
         for piece in range(RING):
             span = pl.ds(piece * width, width)
-
-            @pl.when(section < last)
-            def _():
-                wave_copy(part, piece).wait_recv()
-
+            wave_copy(part, piece).wait_recv()
             left = upstream[rows, span]
             for start, size in tiles(hidden):
                 cols = pl.ds(start, size)
@@ -434,9 +436,21 @@
     for part, (first, count) in enumerate(parts):
         copies.wait_recv(grads.at[pl.ds(tokens + first, count)], ("grads", part))
     both = sides[:, pl.ds(0, 2 * tokens)]
-    for start, size in tiles(2 * hidden):
-        cols = pl.ds(start, size)
-        rail_ref[:, cols] = mm(both, grads[:, cols]).astype(BF16)
+    stores = []
+    for half in (0, 1):
+        for start, size in tiles(hidden):
+            cols = pl.ds(half * hidden + start, size)
+            rail_hold[:, cols] = mm(both, grads[:, cols]).astype(BF16)
+        for number in range(rail // PAD):
+            pack(rail_hold, number * PAD, half * hidden, hidden)
+        cols = pl.ds(half * hidden, hidden)
+        stores.append(
+            pltpu.make_async_copy(rail_hold.at[:, cols], rail_ref.at[:, cols], rail_sem.at[half])
+        )
+        stores[-1].start()
+
+    for store in stores:
+        store.wait()
 
     @pl.when(section > 0)
     def _():
@@ -458,7 +472,7 @@
     return (updated, moment_one, moment_two)
 
 
-def reduce_steps(rail, near, whole, near_last, whole_last, copies, hidden):
+def reduce_steps(rail_ref, rail, near, whole, near_last, whole_last, copies, hidden):
     y, x, core = coords()
 
     def place(half, bulk, other):
@@ -466,9 +480,9 @@
             return (y + bulk) % RING, (x + other) % RING
         return (y + other) % RING, (x + bulk) % RING
 
-    def block(half, bulk, other, which):
+    def block(half, bulk, other, which, ref=rail):
         py, px = place(half, bulk, other)
-        return part_of(rail, (py * RING + px) * PAD, half * hidden, which, hidden)
+        return part_of(ref, (py * RING + px) * PAD, half * hidden, which, hidden)
 
     def send(src, dst, key, half, axis, step):
         py, px = place(half, step, 0) if axis == 0 else place(half, 0, step)
@@ -485,7 +499,7 @@
 
     def far(half, other):
         for which, step in ways(other):
-            send(block(half, 2, other, which), narrow(near.at[half, other, which], which), ("n", half, other, which), half, 0, step)
+            send(block(half, 2, other, which, rail_ref), narrow(near.at[half, other, which], which), ("n", half, other, which), half, 0, step)
 
     def pass_on(half, other):
         for which, step in ways(other):
@@ -554,17 +568,14 @@
     for load in loads:
         load.start()
     plane_barrier()
-    fetch.wait()
-    for number in range(rail.shape[0] // PAD):
-        pack(rail, number * PAD, 0, hidden)
-        pack(rail, number * PAD, hidden, hidden)
     far, pass_on, settle, far_last, pass_last, total = reduce_steps(
-        rail, near, whole, near_last, whole_last, copies, hidden
+        rail_ref, rail, near, whole, near_last, whole_last, copies, hidden
     )
     order = (2, 1, 3, 0)
     for other in order:
         far(0, other)
         far(1, other)
+    fetch.wait()
     pad_matrix(spread, 1)
     widened, inverse = rms(next_ref[...])
     next_normed = (widened * inverse * gain_ref[...]).astype(BF16)
@@ -735,7 +746,7 @@
             jax.ShapeDtypeStruct((rail_rows, 2 * hidden), BF16),
         ),
         in_specs=[VMEM, VMEM, VMEM, VMEM, VMEM, SMEM, ANY],
-        out_specs=(VMEM, VMEM),
+        out_specs=(VMEM, HBM),
         scratch_shapes=[
             pltpu.VMEM((padded, 2 * hidden), BF16),
             pltpu.VMEM((2 * hidden, padded), BF16),
@@ -755,11 +766,13 @@
             pltpu.VMEM((2 * tokens, 2 * hidden), BF16),
             pltpu.VMEM((rail_rows, 3 * tokens), BF16),
             pltpu.VMEM((PAD, 2 * hidden), BF16),
+            pltpu.VMEM((rail_rows, 2 * hidden), BF16),
             dma((160,)),
             dma((160,)),
             dma((len(PARTS) * RING,)),
             dma((len(PARTS) * RING,)),
             dma(()),
+            dma((2,)),
         ],
         compiler_params=pltpu.CompilerParams(
             collective_id=0, has_side_effects=True, vmem_limit_bytes=60 * 2**20
@@ -780,7 +793,7 @@
         )
         + (row,) * 6
         + (jax.ShapeDtypeStruct((1, 2), F32),),
-        in_specs=[ANY] + [VMEM] * 3 + [ANY] * 6,
+        in_specs=[HBM] + [VMEM] * 3 + [ANY] * 6,
         out_specs=(VMEM,) * 2 + (ANY,) * 6 + (VMEM,),
         scratch_shapes=[
             pltpu.VMEM((padded, 2 * hidden), BF16),

time: 185 us -> 182 us (0.984)
  Pallas kernels: 181 us -> 178 us
where the time goes in v3:
time: 182 us; the launch traced here: 179 us
  Pallas kernels  178 us (98%)
    pallas_call x1, Pallas kernels, shards(): pl.pallas_call(back_kernel, out_shape=(jax.ShapeDtypeStruct((tokens, padd...  110 us
    pallas_call x1, Pallas kernels, shards(): pl.pallas_call(update_kernel, out_shape=(jax.ShapeDtypeStruct((tokens, fe...  63.6 us
    pallas_call x1, Pallas kernels, shards(): pl.pallas_call(functools.partial(deliver_kernel, len(outs)), out_shape=tu...  4.31 us

profile of v3, /device:TPU:1, one launch (start us, length us, event | category | flops | bytes accessed | tf_op | source)
XLA Modules:
  0.0 178.8 jit_solution(15749860355414362277)
XLA Ops:
  0.6 110.0 %shard_map.205 = (bf16[256,1024]{1,0:T(8,128)(2,1)}, bf16[512,4864]{1,0:T(8,128)(2,1)}) custom-call(bf16[28,2432]{1,0:T(8,128)(2,1)} %bitcast.28, bf16[28,2432]{1,0:T(8,128)(2,1)} %bitcast.29, bf16[256,896]{1,0:T(8,128)(2,1)} %bitcast.20, bf16[256,896]{1,0:T(8,128)(2,1)} %cot_ref.1, f32[1,896]{1,0:T(1,128)} %gain_ref.3, f32[1,2]{1,0:T(1,128)} %scale_ref.1, ...), custom_call_target="tpu_custom_call" | custom-call | tf_op jit(solution)/shard_map/pallas_call | solution.py:742
  110.7 63.6 %shard_map.206 = (bf16[256,896]{1,0:T(8,128)(2,1)}, bf16[256,2432]{1,0:T(8,128)(2,1)}, f32[532,1,128]{2,1,0:T(1,128)}, f32[532,1,128]{2,1,0:T(1,128)}, f32[532,1...) custom-call(bf16[512,4864]{1,0:T(8,128)(2,1)} %get-tuple-element.29., ...), custom_call_target="tpu_custom_call" | custom-call | tf_op jit(solution)/shard_map/pallas_call | solution.py:788
  174.2 4.3 %shard_map.207 = (bf16[256,896]{1,0:T(8,128)(2,1)}, bf16[256,2432]{1,0:T(8,128)(2,1)}, f32[532,1,128]{2,1,0:T(1,128)}, f32[532,1,128]{2,1,0:T(1,128)}, f32[532,1...) custom-call(bf16[256,896]{1,0:T(8,128)(2,1)} %get-tuple-element.31.r, ...), custom_call_target="tpu_custom_call" | custom-call | tf_op jit(solution)/shard_map/pallas_call | solution.py:823
